TPU v7x, 32 devices: a whole 2x2x4 slice. The times are simulated.
32 devices in a mesh: member: 2 (over y), lon: 4 (over z), lat: 2 (over x), dp: 2 (over core).
Axes of the slice: x: 2, y: 2, z: 4, core: 2. Of those that a mesh axis runs over, the one named last changes fastest.
Arguments:
- fields: bfloat16 [4, 64, 32, 512], P(('member', 'dp'), 'lat', 'lon'), parts along dimension 0, may hold values from -6 to 6
- cotangent: bfloat16 [4, 64, 32, 512], P(('member', 'dp'), 'lat', 'lon'), parts along dimension 0, may hold values from -6 to 6
- conv_weight: float32 [7, 7, 512], replicated, may hold values from -0.875 to 0.875
- norm_gain: float32 [512], replicated, may hold values from 0.1 to 1.9
- w_qkv: bfloat16 [512, 768], replicated, may hold values from -1 to 1
- w_out: bfloat16 [256, 512], replicated, may hold values from -0.375 to 0.375
Outputs:
- result: bfloat16 [4, 64, 32, 512], P(('member', 'dp'), 'lat', 'lon'), parts along dimension 0
- grad_fields: bfloat16 [4, 64, 32, 512], P(('member', 'dp'), 'lat', 'lon'), parts along dimension 0
- grad_qkv: float32 [1024, 768], P('member'), parts along dimension 0
- grad_out: float32 [512, 512], P('member'), parts along dimension 0
- grad_conv: float32 [14, 7, 512], P('member'), parts along dimension 0
- grad_gain: float32 [1024], P('member'), parts along dimension 0
There are 2 independent parts, one for each index of `member`. A program takes and returns all parts, laid end to end along the dimension named above; an argument that names none is the same for every part. Nothing has to cross between parts.
All inputs are finite; a program needn't handle non-finite values.
Results may differ from a plain program's by a relative error of at most 0.012.
The roundings to bfloat16 on the way count: a program that leaves them out, or rounds other values in their place, can miss the bound.
Values may be sent and summed in bfloat16 or wider, within the bound.
A program may use at most 64 MiB of HBM per device.

v0:
```python
import jax
import jax.numpy as jnp
from jax import lax
from jax.sharding import PartitionSpec as P

HEADS = 4
HEAD_DIM = 64
EPSILON = 1e-06


def with_halo(x, sides, width, wrap):
    for axis, dim in sides:
        size, length = (lax.axis_size(axis), x.shape[dim])
        up = [(i, (i + 1) % size) for i in range(size if wrap else size - 1)]
        down = [(j, i) for i, j in up]
        last = lax.slice_in_dim(x, length - width, length, axis=dim)
        first = lax.slice_in_dim(x, 0, width, axis=dim)
        before = lax.ppermute(last, axis, up)
        after = lax.ppermute(first, axis, down)
        x = jnp.concatenate([before, x, after], axis=dim)
    return x


def spread(padded, kernel, lat_rows, lon_cols):
    summed = jnp.zeros(padded.shape[:1] + (lat_rows, lon_cols, padded.shape[3]), jnp.float32)
    for row_shift in range(7):
        band = padded[:, row_shift : row_shift + lat_rows].astype(jnp.float32)
        partial_row = kernel[row_shift, 0] * band[:, :, 0:lon_cols]
        for col_shift in range(1, 7):
            partial_row = (
                partial_row
                + kernel[row_shift, col_shift] * band[:, :, col_shift : col_shift + lon_cols]
            )
        summed = summed + partial_row
    return summed


def correlate(padded, upstream, lat_rows, lon_cols):
    pieces = []
    for row_shift in range(7):
        for col_shift in range(7):
            window = padded[
                :, row_shift : row_shift + lat_rows, col_shift : col_shift + lon_cols
            ].astype(jnp.float32)
            pieces.append(jnp.sum(window * upstream, axis=(0, 1, 2)))
    return jnp.stack(pieces).reshape(7, 7, -1)


def split_heads(values):
    return values.reshape(values.shape[:-1] + (HEADS, HEAD_DIM))


def attend_forward(rowwise, att_width):
    queries = split_heads(rowwise[..., :att_width])
    keys_part = split_heads(rowwise[..., att_width : 2 * att_width])
    values_part = split_heads(rowwise[..., 2 * att_width :])
    scores = jnp.einsum(
        "brqhd,brkhd->brhqk", queries, keys_part, preferred_element_type=jnp.float32
    ) * HEAD_DIM ** (-0.5)
    row_peak = jnp.max(scores, -1, keepdims=True)
    raised = jnp.exp(scores - row_peak)
    probs = raised / jnp.sum(raised, -1, keepdims=True)
    weights = probs.astype(jnp.bfloat16)
    mixed = jnp.einsum(
        "brhqk,brkhd->brqhd", weights, values_part, preferred_element_type=jnp.float32
    )
    return (mixed.reshape(rowwise.shape[:3] + (att_width,)).astype(jnp.bfloat16), probs)


def attend_backward(rowwise, probs, grad_rowwise, att_width):
    queries = split_heads(rowwise[..., :att_width])
    keys_part = split_heads(rowwise[..., att_width : 2 * att_width])
    values_part = split_heads(rowwise[..., 2 * att_width :])
    grad_heads = split_heads(grad_rowwise)
    weights = probs.astype(jnp.bfloat16)
    grad_probs = jnp.einsum(
        "brqhd,brkhd->brhqk", grad_heads, values_part, preferred_element_type=jnp.float32
    )
    inner = jnp.sum(probs * grad_probs, -1, keepdims=True)
    grad_scores = (probs * (grad_probs - inner) * HEAD_DIM ** (-0.5)).astype(jnp.bfloat16)
    grad_query = jnp.einsum(
        "brhqk,brkhd->brqhd", grad_scores, keys_part, preferred_element_type=jnp.float32
    )
    grad_key = jnp.einsum(
        "brhqk,brqhd->brkhd", grad_scores, queries, preferred_element_type=jnp.float32
    )
    grad_value = jnp.einsum(
        "brhqk,brqhd->brkhd", weights, grad_heads, preferred_element_type=jnp.float32
    )
    shaped = rowwise.shape[:3] + (att_width,)
    return jnp.concatenate(
        [
            grad_query.reshape(shaped).astype(jnp.bfloat16),
            grad_key.reshape(shaped).astype(jnp.bfloat16),
            grad_value.reshape(shaped).astype(jnp.bfloat16),
        ],
        axis=-1,
    )


def contract_rows(left, right):
    return lax.dot_general(
        left, right, (((0,), (0,)), ((), ())), preferred_element_type=jnp.float32
    )


def contract_cols(left, right):
    return lax.dot_general(
        left, right, (((1,), (1,)), ((), ())), preferred_element_type=jnp.float32
    )


def on_device(fields, cotangent, conv_weight, norm_gain, w_qkv, w_out):
    batch_count, lat_rows, lon_cols, channels = fields.shape
    att_width = w_out.shape[0]
    wide = with_halo(fields, (("lon", 2),), 3, True)
    padded = with_halo(wide, (("lat", 1),), 3, False)
    update = fields.astype(jnp.float32) + spread(padded, conv_weight, lat_rows, lon_cols)
    inverse = lax.rsqrt(jnp.mean(update * update, -1, keepdims=True) + EPSILON)
    normed = (update * inverse * norm_gain).astype(jnp.bfloat16)
    normed_flat = normed.reshape(-1, channels)
    projected = jnp.dot(normed_flat, w_qkv, preferred_element_type=jnp.float32).astype(jnp.bfloat16)
    rowwise = lax.all_to_all(
        projected.reshape(batch_count, lat_rows, lon_cols, 3 * att_width),
        "lon",
        split_axis=1,
        concat_axis=2,
        tiled=True,
    )
    mixed_rows, probs = attend_forward(rowwise, att_width)
    mixed = lax.all_to_all(mixed_rows, "lon", split_axis=2, concat_axis=1, tiled=True)
    mixed_flat = mixed.reshape(-1, att_width)
    result = (
        update
        + jnp.dot(mixed_flat, w_out, preferred_element_type=jnp.float32).reshape(update.shape)
    ).astype(jnp.bfloat16)
    upstream_flat = cotangent.reshape(-1, channels)
    grad_mixed = contract_cols(upstream_flat, w_out).astype(jnp.bfloat16)
    grad_out = contract_rows(mixed_flat, upstream_flat)
    grad_rowwise = lax.all_to_all(
        grad_mixed.reshape(batch_count, lat_rows, lon_cols, att_width),
        "lon",
        split_axis=1,
        concat_axis=2,
        tiled=True,
    )
    grad_projected_rows = attend_backward(rowwise, probs, grad_rowwise, att_width)
    grad_projected = lax.all_to_all(
        grad_projected_rows, "lon", split_axis=2, concat_axis=1, tiled=True
    )
    grad_flat = grad_projected.reshape(-1, 3 * att_width)
    grad_weight = contract_rows(normed_flat, grad_flat)
    grad_normed = contract_cols(grad_flat, w_qkv).reshape(update.shape)
    grad_gain = jnp.sum(grad_normed * (update * inverse), axis=(0, 1, 2))
    gained = norm_gain * grad_normed
    grad_update = (
        cotangent.astype(jnp.float32)
        + inverse * gained
        - update * inverse**3 * jnp.mean(gained * update, -1, keepdims=True)
    )
    grad_wide = with_halo(grad_update.astype(jnp.bfloat16), (("lon", 2),), 3, True).astype(
        grad_update.dtype
    )
    grad_padded = with_halo(grad_wide.astype(jnp.bfloat16), (("lat", 1),), 3, False).astype(
        grad_wide.dtype
    )
    grad_fields = (
        grad_update + spread(grad_padded, conv_weight[::-1, ::-1], lat_rows, lon_cols)
    ).astype(jnp.bfloat16)
    grad_conv = correlate(padded, grad_update, lat_rows, lon_cols)
    totals = lax.psum((grad_weight, grad_out, grad_conv, grad_gain), ("lon", "lat", "dp"))
    return (result, grad_fields, totals[0], totals[1], totals[2], totals[3])


def solution(mesh):
    placed = (
        P(("member", "dp"), "lat", "lon", None),
        P(("member", "dp"), "lat", "lon", None),
        P(),
        P(),
        P(),
        P(),
    )
    return jax.shard_map(
        on_device,
        mesh=mesh,
        in_specs=placed,
        out_specs=(
            P(("member", "dp"), "lat", "lon", None),
            P(("member", "dp"), "lat", "lon", None),
            P("member", None),
            P("member", None),
            P("member", None, None),
            P("member"),
        ),
        check_vma=False,
    )
```

profile of v0, /device:TPU:0, one launch (start us, length us, event | category | flops | bytes accessed | tf_op | source)
XLA Modules:
  0.0 233.1 jit_solution(6971295654083758024)
XLA Ops:
  8.4 3.1 %collective-permute-start = (bf16[1,32,3,512]{3,2,1,0:T(4,128)(2,1)S(1)}, bf16[1,32,3,512]{3,2,1,0:T(4,128)(2,1)S(1)}, u32[]{:S(2)}, u32[]{:S(2)}) collective-permute-start(bf16[1,32,3,512]{3,2,1,0:T(4,128)(2,1)S(1)} %get-tuple-element.93), channel_id=1, source_target_pairs={{0,4},{4,8},{8,12},{12,0},{1,5},{5,9},{9,13},{13,1},{2,6},{6,10},{... | collective-permute-start | bytes 294920 | tf_op jit(solution)/shard_map/ppermute | solution.py:18
  11.6 2.1 collective-permute-start.1
  13.6 1.9 fusion.15
  15.6 3.9 %all-to-all-start.2 = ((bf16[1,32,8,256]{3,2,0,1:T(8,128)(2,1)}), bf16[1,32,8,256]{3,2,0,1:T(8,128)(2,1)}, u32[]{:S(2)}, u32[]{:S(2)}) async-start(bf16[1,32,8,256]{3,2,0,1:T(8,128)(2,1)} %fusion.15), calls=%async_computation.2 | async-start | bytes 262144 | tf_op jit(solution)/shard_map/all_to_all | solution.py:140
  22.1 3.5 %collective-permute-start.2 = (bf16[1,3,14,512]{3,2,1,0:T(8,128)(2,1)S(1)}, bf16[1,3,14,512]{3,2,1,0:T(8,128)(2,1)S(1)}, u32[]{:S(2)}, u32[]{:S(2)}) collective-permute-start(bf16[1,3,14,512]{3,2,1,0:T(8,128)(2,1)S(1)} %get-tuple-element.84), channel_id=1, source_target_pairs={{0,2},{1,3},{4,6},{5,7},{8,10},{9,11},{12,14},{13,15},{16,18},{17,... | collective-permute-start | bytes 129032 | tf_op jit(solution)/shard_map/ppermute | solution.py:18
  25.7 1.3 collective-permute-start.3
  27.6 4.0 %collective-permute-done.3 = bf16[1,3,14,512]{3,2,1,0:T(8,128)(2,1)S(1)} collective-permute-done((bf16[1,3,14,512]{3,2,1,0:T(8,128)(2,1)S(1)}, bf16[1,3,14,512]{3,2,1,0:T(8,128)(2,1)S(1)}, u32[]{:S(2)}, u32[]{:S(2)}) %collective-permute-start.3) | collective-permute-done | bytes 43040 | tf_op jit(solution)/shard_map/ppermute | solution.py:19
  32.0 2.0 slice_convert_fusion.2
  34.0 10.5 %multiply_reduce_fusion.51 = (f32[32,8]{1,0:T(8,128)S(1)}, f32[1,32,8,512]{3,2,1,0:T(8,128)S(1)}) fusion(f32[1,32,14,512]{3,2,1,0:T(8,128)S(1)} %get-tuple-element.77, f32[512]{0:T(512)} %bitcast.283, f32[512]{0:T(512)} %bitcast.285, f32[512]{0:T(512)S(1)} %bitcast.191, f32[512]{0:T(512)S(1)} %bitcast.193, f32[512]{0:T(512)S(1)} %bitcast.195, ...), kind=kLoop, calls=%fused_computation.293 | loop fusion | flops 13238016 | bytes 26577920 | tf_op jit(solution)/shard_map/reduce_sum | solution.py:119
  45.7 5.0 %all-to-all-start = ((bf16[1,32,8,768]{3,2,0,1:T(8,128)(2,1)}), bf16[1,32,8,768]{3,2,0,1:T(8,128)(2,1)S(1)}, u32[]{:S(2)}, u32[]{:S(2)}) async-start(bf16[1,32,8,768]{3,2,0,1:T(8,128)(2,1)} %fusion.10), calls=%async_computation | async-start | bytes 786432 | tf_op jit(solution)/shard_map/all_to_all | solution.py:123
  51.5 1.6 copy.83
  54.2 6.2 %all-to-all-done = bf16[1,32,8,768]{3,2,0,1:T(8,128)(2,1)S(1)} async-done(((bf16[1,32,8,768]{3,2,0,1:T(8,128)(2,1)}), bf16[1,32,8,768]{3,2,0,1:T(8,128)(2,1)S(1)}, u32[]{:S(2)}, u32[]{:S(2)}) %all-to-all-start) | async-done | bytes 393248 | tf_op jit(solution)/shard_map/all_to_all | solution.py:123
  62.3 2.1 fusion.164
  65.5 2.0 fusion.14
  68.6 2.6 %fusion.12 = bf16[1,8,32,4,64]{4,2,3,1,0:T(8,128)(2,1)} fusion(f32[8,4,32,32]{2,3,1,0:T(8,128)} %fusion.129, bf16[8,32,4,64]{3,2,1,0:T(4,128)(2,1)S(1)} %copy-done.18, f32[8,4,32,32]{2,3,1,0:T(8,128)} %get-tuple-element.147, f32[8,4,32]{2,1,0:T(4,128)S(1)} %get-tuple-element.146), kind=kOutput, calls=%fused_computation.20 | convolution fusion | flops 4490271 | bytes 528384 | tf_op jit(solution)/shard_map/brhqk,brkhd->brqhd/dot_general | solution.py:81
  75.1 3.9 %all-to-all-start.1 = ((bf16[1,8,32,256]{3,1,0,2:T(8,128)(2,1)}), bf16[1,8,32,256]{3,1,0,2:T(8,128)(2,1)}, u32[]{:S(2)}, u32[]{:S(2)}) async-start(bf16[1,8,32,256]{3,1,0,2:T(8,128)(2,1)} %reshape.619), calls=%async_computation.1 | async-start | bytes 262144 | tf_op jit(solution)/shard_map/all_to_all | solution.py:131
  79.1 2.6 %fusion.13 = bf16[1,8,32,4,64]{4,2,3,1,0:T(8,128)(2,1)} fusion(f32[8,4,32,32]{2,3,1,0:T(8,128)} %fusion.129, bf16[8,32,4,64]{3,2,1,0:T(4,128)(2,1)S(1)} %copy-done.17, f32[8,4,32,32]{2,3,1,0:T(8,128)} %get-tuple-element.147, f32[8,4,32]{2,1,0:T(4,128)S(1)} %get-tuple-element.146), kind=kOutput, calls=%fused_computation.21 | convolution fusion | flops 4490271 | bytes 528384 | tf_op jit(solution)/shard_map/brhqk,brqhd->brkhd/dot_general | solution.py:84
  87.6 5.0 %all-to-all-start.3 = ((bf16[1,8,32,768]{3,1,0,2:T(8,128)(2,1)}), bf16[1,8,32,768]{3,1,0,2:T(8,128)(2,1)S(1)}, u32[]{:S(2)}, u32[]{:S(2)}) async-start(bf16[1,8,32,768]{3,1,0,2:T(8,128)(2,1)} %copy.93), calls=%async_computation.3 | async-start | bytes 786432 | tf_op jit(solution)/shard_map/all_to_all | solution.py:148
  92.7 1.7 constant_dynamic-update-slice_fusion
  97.3 4.3 %all-to-all-done.3 = bf16[1,8,32,768]{3,1,0,2:T(8,128)(2,1)S(1)} async-done(((bf16[1,8,32,768]{3,1,0,2:T(8,128)(2,1)}), bf16[1,8,32,768]{3,1,0,2:T(8,128)(2,1)S(1)}, u32[]{:S(2)}, u32[]{:S(2)}) %all-to-all-start.3) | async-done | bytes 393248 | tf_op jit(solution)/shard_map/all_to_all | solution.py:148
  102.7 2.2 multiply_reduce_fusion.2
  104.9 2.0 multiply_reduce_fusion.29
  107.6 3.3 %collective-permute-start.5 = (bf16[1,32,3,512]{3,2,1,0:T(4,128)(2,1)S(1)}, bf16[1,32,3,512]{3,2,1,0:T(4,128)(2,1)S(1)}, u32[]{:S(2)}, u32[]{:S(2)}) collective-permute-start(bf16[1,32,3,512]{3,2,1,0:T(4,128)(2,1)S(1)} %get-tuple-element.92), channel_id=1, source_target_pairs={{4,0},{8,4},{12,8},{0,12},{5,1},{9,5},{13,9},{1,13},{6,2},{10,6},{... | collective-permute-start | bytes 294920 | tf_op jit(solution)/shard_map/ppermute | solution.py:19
  110.9 1.7 multiply_reduce_fusion.20
  112.6 1.4 collective-permute-done.4
  114.1 1.9 collective-permute-start.6
  116.3 1.3 collective-permute-start.7
  117.6 1.6 fusion.139
  121.2 31.5 %psum.31 = f32[512]{0:T(512)} all-reduce(f32[512]{0:T(512)S(1)} %copy-done.93), channel_id=1, replica_groups=mesh['member'=2,'lon'=4,'lat'=2,'dp'=2] {'lon','lat','dp'}, use_global_device_ids=true, to_apply=%region_58.0 | all-reduce | flops 512 | bytes 4096 | tf_op jit(solution)/shard_map/psum | solution.py:171
  153.3 4.5 %fusion.24 = bf16[1,32,8,512]{3,2,1,0:T(8,128)(2,1)} fusion(f32[1,32,8,512]{3,2,1,0:T(8,128)S(1)} %get-tuple-element.70, f32[1,38,14,512]{3,2,1,0:T(8,128)S(1)} %maximum_convert_fusion, f32[512]{0:T(512)S(1)} %bitcast.284, f32[512]{0:T(512)S(1)} %bitcast.286, f32[512]{0:T(512)S(1)} %bitcast.192, f32[512]{0:T(512)S(1)} %bitcast.194, f32[512]{0:T(512)S(1)} %bitcast.196, ...), kind=kLoop, calls=%fused_computation.42 | loop fusion | flops 12976128 | bytes 26576896 | tf_op jit(solution)/shard_map/convert_element_type | solution.py:169
  157.8 64.3 %all-reduce.3.cloned.1.call-done = (f32[512,768]{1,0:T(8,128)}, f32[256,512]{1,0:T(8,128)}, f32[7,7,512]{2,1,0:T(8,128)}) async-done(((f32[512,768]{1,0:T(8,128)}, f32[256,512]{1,0:T(8,128)}, f32[7,7,512]{2,1,0:T(8,128)}), (f32[512,768]{1,0:T(8,128)}, f32[256,512]{1,0:T(8,128)}, f32[7,7,512]{2,1,0:T(8,128)})) %all-reduce.3.cloned.1.call-update) | async-done | bytes 2197520 | tf_op jit(solution)/shard_map/psum | solution.py:171
  222.1 2.7 %copy.139 = f32[512,768]{1,0:T(8,128)} copy(f32[512,768]{1,0:T(8,128)} %get-tuple-element.154) | data formatting | bytes 3145728
  (244 shorter events, 29.8 us)
Async XLA Ops:
  7.2 37.4 %copy-start = (bf16[512,768]{1,0:T(8,128)(2,1)S(1)}, bf16[512,768]{1,0:T(8,128)(2,1)}, u32[]{:S(2)}) copy-start(bf16[512,768]{1,0:T(8,128)(2,1)} %param.10) | copy-start | bytes 2359300
  8.4 12.4 %collective-permute-start = (bf16[1,32,3,512]{3,2,1,0:T(4,128)(2,1)S(1)}, bf16[1,32,3,512]{3,2,1,0:T(4,128)(2,1)S(1)}, u32[]{:S(2)}, u32[]{:S(2)}) collective-permute-start(bf16[1,32,3,512]{3,2,1,0:T(4,128)(2,1)S(1)} %get-tuple-element.93), channel_id=1, source_target_pairs={{0,4},{4,8},{8,12},{12,0},{1,5},{5,9},{9,13},{13,1},{2,6},{6,10},{... | collective-permute-start | bytes 294920 | tf_op jit(solution)/shard_map/ppermute | solution.py:18
  11.6 9.3 %collective-permute-start.1 = (bf16[1,32,3,512]{3,2,1,0:T(4,128)(2,1)S(1)}, bf16[1,32,3,512]{3,2,1,0:T(4,128)(2,1)S(1)}, u32[]{:S(2)}, u32[]{:S(2)}) collective-permute-start(bf16[1,32,3,512]{3,2,1,0:T(4,128)(2,1)S(1)} %get-tuple-element.94), channel_id=1, source_target_pairs={{4,0},{8,4},{12,8},{0,12},{5,1},{9,5},{13,9},{1,13},{6,2},{10,6},{... | collective-permute-start | bytes 294920 | tf_op jit(solution)/shard_map/ppermute | solution.py:19
  15.6 30.2 %all-to-all-start.2 = ((bf16[1,32,8,256]{3,2,0,1:T(8,128)(2,1)}), bf16[1,32,8,256]{3,2,0,1:T(8,128)(2,1)}, u32[]{:S(2)}, u32[]{:S(2)}) async-start(bf16[1,32,8,256]{3,2,0,1:T(8,128)(2,1)} %fusion.15), calls=%async_computation.2 | async-start | bytes 262144 | tf_op jit(solution)/shard_map/all_to_all | solution.py:140
  22.1 5.5 %collective-permute-start.2 = (bf16[1,3,14,512]{3,2,1,0:T(8,128)(2,1)S(1)}, bf16[1,3,14,512]{3,2,1,0:T(8,128)(2,1)S(1)}, u32[]{:S(2)}, u32[]{:S(2)}) collective-permute-start(bf16[1,3,14,512]{3,2,1,0:T(8,128)(2,1)S(1)} %get-tuple-element.84), channel_id=1, source_target_pairs={{0,2},{1,3},{4,6},{5,7},{8,10},{9,11},{12,14},{13,15},{16,18},{17,... | collective-permute-start | bytes 129032 | tf_op jit(solution)/shard_map/ppermute | solution.py:18
  25.7 6.0 %collective-permute-start.3 = (bf16[1,3,14,512]{3,2,1,0:T(8,128)(2,1)S(1)}, bf16[1,3,14,512]{3,2,1,0:T(8,128)(2,1)S(1)}, u32[]{:S(2)}, u32[]{:S(2)}) collective-permute-start(bf16[1,3,14,512]{3,2,1,0:T(8,128)(2,1)S(1)} %get-tuple-element.85), channel_id=1, source_target_pairs={{2,0},{3,1},{6,4},{7,5},{10,8},{11,9},{14,12},{15,13},{18,16},{19,... | collective-permute-start | bytes 129032 | tf_op jit(solution)/shard_map/ppermute | solution.py:19
  45.7 14.6 %all-to-all-start = ((bf16[1,32,8,768]{3,2,0,1:T(8,128)(2,1)}), bf16[1,32,8,768]{3,2,0,1:T(8,128)(2,1)S(1)}, u32[]{:S(2)}, u32[]{:S(2)}) async-start(bf16[1,32,8,768]{3,2,0,1:T(8,128)(2,1)} %fusion.10), calls=%async_computation | async-start | bytes 786432 | tf_op jit(solution)/shard_map/all_to_all | solution.py:123
  75.1 12.5 %all-to-all-start.1 = ((bf16[1,8,32,256]{3,1,0,2:T(8,128)(2,1)}), bf16[1,8,32,256]{3,1,0,2:T(8,128)(2,1)}, u32[]{:S(2)}, u32[]{:S(2)}) async-start(bf16[1,8,32,256]{3,1,0,2:T(8,128)(2,1)} %reshape.619), calls=%async_computation.1 | async-start | bytes 262144 | tf_op jit(solution)/shard_map/all_to_all | solution.py:131
  87.6 13.9 %all-to-all-start.3 = ((bf16[1,8,32,768]{3,1,0,2:T(8,128)(2,1)}), bf16[1,8,32,768]{3,1,0,2:T(8,128)(2,1)S(1)}, u32[]{:S(2)}, u32[]{:S(2)}) async-start(bf16[1,8,32,768]{3,1,0,2:T(8,128)(2,1)} %copy.93), calls=%async_computation.3 | async-start | bytes 786432 | tf_op jit(solution)/shard_map/all_to_all | solution.py:148
  92.7 129.4 %all-reduce.3.cloned.1.call-start = ((), (), s32[]{:S(2)}) async-start(), calls=%async_computation.4 | async-start | bytes 4423680 | tf_op jit(solution)/shard_map/psum | solution.py:171
  107.0 6.9 %collective-permute-start.4 = (bf16[1,32,3,512]{3,2,1,0:T(4,128)(2,1)S(1)}, bf16[1,32,3,512]{3,2,1,0:T(4,128)(2,1)S(1)}, u32[]{:S(2)}, u32[]{:S(2)}) collective-permute-start(bf16[1,32,3,512]{3,2,1,0:T(4,128)(2,1)S(1)} %get-tuple-element.91), channel_id=1, source_target_pairs={{0,4},{4,8},{8,12},{12,0},{1,5},{5,9},{9,13},{13,1},{2,6},{6,10},{... | collective-permute-start | bytes 294920 | tf_op jit(solution)/shard_map/ppermute | solution.py:18
  107.6 6.4 %collective-permute-start.5 = (bf16[1,32,3,512]{3,2,1,0:T(4,128)(2,1)S(1)}, bf16[1,32,3,512]{3,2,1,0:T(4,128)(2,1)S(1)}, u32[]{:S(2)}, u32[]{:S(2)}) collective-permute-start(bf16[1,32,3,512]{3,2,1,0:T(4,128)(2,1)S(1)} %get-tuple-element.92), channel_id=1, source_target_pairs={{4,0},{8,4},{12,8},{0,12},{5,1},{9,5},{13,9},{1,13},{6,2},{10,6},{... | collective-permute-start | bytes 294920 | tf_op jit(solution)/shard_map/ppermute | solution.py:19
  114.1 38.6 %collective-permute-start.6 = (bf16[1,3,14,512]{3,2,1,0:T(8,128)(2,1)S(1)}, bf16[1,3,14,512]{3,2,1,0:T(8,128)(2,1)S(1)}, u32[]{:S(2)}, u32[]{:S(2)}) collective-permute-start(bf16[1,3,14,512]{3,2,1,0:T(8,128)(2,1)S(1)} %get-tuple-element.80), channel_id=1, source_target_pairs={{0,2},{1,3},{4,6},{5,7},{8,10},{9,11},{12,14},{13,15},{16,18},{17,... | collective-permute-start | bytes 129032 | tf_op jit(solution)/shard_map/ppermute | solution.py:18
  116.3 36.4 %collective-permute-start.7 = (bf16[1,3,14,512]{3,2,1,0:T(8,128)(2,1)S(1)}, bf16[1,3,14,512]{3,2,1,0:T(8,128)(2,1)S(1)}, u32[]{:S(2)}, u32[]{:S(2)}) collective-permute-start(bf16[1,3,14,512]{3,2,1,0:T(8,128)(2,1)S(1)} %get-tuple-element.81), channel_id=1, source_target_pairs={{2,0},{3,1},{6,4},{7,5},{10,8},{11,9},{14,12},{15,13},{18,16},{19,... | collective-permute-start | bytes 129032 | tf_op jit(solution)/shard_map/ppermute | solution.py:19
  119.8 32.8 %copy-start.4 = (bf16[1,32,8,512]{3,2,1,0:T(8,128)(2,1)S(1)}, bf16[1,32,8,512]{3,2,1,0:T(8,128)(2,1)}, u32[]{:S(2)}) copy-start(bf16[1,32,8,512]{3,2,1,0:T(8,128)(2,1)} %copy-done.3) | copy-start | bytes 786436
  119.8 32.8 %copy-start.13 = (bf16[1,32,3,512]{3,2,1,0:T(4,128)(2,1)S(1)}, bf16[1,32,3,512]{3,2,1,0:T(4,128)(2,1)}, u32[]{:S(2)}) copy-start(bf16[1,32,3,512]{3,2,1,0:T(4,128)(2,1)} %copy-done.12) | copy-start | bytes 294916
  119.8 32.8 %copy-start.15 = (bf16[1,32,3,512]{3,2,1,0:T(4,128)(2,1)S(1)}, bf16[1,32,3,512]{3,2,1,0:T(4,128)(2,1)}, u32[]{:S(2)}) copy-start(bf16[1,32,3,512]{3,2,1,0:T(4,128)(2,1)} %copy-done.14) | copy-start | bytes 294916
  120.5 32.4 %copy-start.22 = (f32[1,1,512]{2,1,0:T(1,128)S(1)}, f32[1,1,512]{2,1,0:T(1,128)}, u32[]{:S(2)}) copy-start(f32[1,1,512]{2,1,0:T(1,128)} %get-tuple-element.108) | copy-start | bytes 6148
  120.6 32.4 %copy-start.23 = (f32[1,1,512]{2,1,0:T(1,128)S(1)}, f32[1,1,512]{2,1,0:T(1,128)}, u32[]{:S(2)}) copy-start(f32[1,1,512]{2,1,0:T(1,128)} %get-tuple-element.109) | copy-start | bytes 6148
  120.6 32.4 %copy-start.24 = (f32[1,1,512]{2,1,0:T(1,128)S(1)}, f32[1,1,512]{2,1,0:T(1,128)}, u32[]{:S(2)}) copy-start(f32[1,1,512]{2,1,0:T(1,128)} %get-tuple-element.110) | copy-start | bytes 6148
  120.6 32.4 %copy-start.25 = (f32[1,1,512]{2,1,0:T(1,128)S(1)}, f32[1,1,512]{2,1,0:T(1,128)}, u32[]{:S(2)}) copy-start(f32[1,1,512]{2,1,0:T(1,128)} %get-tuple-element.111) | copy-start | bytes 6148
  120.6 32.4 %copy-start.26 = (f32[1,1,512]{2,1,0:T(1,128)S(1)}, f32[1,1,512]{2,1,0:T(1,128)}, u32[]{:S(2)}) copy-start(f32[1,1,512]{2,1,0:T(1,128)} %get-tuple-element.112) | copy-start | bytes 6148
  120.6 32.4 %copy-start.27 = (f32[1,1,512]{2,1,0:T(1,128)S(1)}, f32[1,1,512]{2,1,0:T(1,128)}, u32[]{:S(2)}) copy-start(f32[1,1,512]{2,1,0:T(1,128)} %get-tuple-element.113) | copy-start | bytes 6148
  120.6 32.4 %copy-start.28 = (f32[1,1,512]{2,1,0:T(1,128)S(1)}, f32[1,1,512]{2,1,0:T(1,128)}, u32[]{:S(2)}) copy-start(f32[1,1,512]{2,1,0:T(1,128)} %get-tuple-element.114) | copy-start | bytes 6148
  120.6 32.4 %copy-start.29 = (f32[1,1,512]{2,1,0:T(1,128)S(1)}, f32[1,1,512]{2,1,0:T(1,128)}, u32[]{:S(2)}) copy-start(f32[1,1,512]{2,1,0:T(1,128)} %get-tuple-element.115) | copy-start | bytes 6148
  120.6 32.4 %copy-start.30 = (f32[1,1,512]{2,1,0:T(1,128)S(1)}, f32[1,1,512]{2,1,0:T(1,128)}, u32[]{:S(2)}) copy-start(f32[1,1,512]{2,1,0:T(1,128)} %get-tuple-element.116) | copy-start | bytes 6148
  120.6 32.4 %copy-start.31 = (f32[1,1,512]{2,1,0:T(1,128)S(1)}, f32[1,1,512]{2,1,0:T(1,128)}, u32[]{:S(2)}) copy-start(f32[1,1,512]{2,1,0:T(1,128)} %get-tuple-element.117) | copy-start | bytes 6148
  120.6 32.4 %copy-start.32 = (f32[1,1,512]{2,1,0:T(1,128)S(1)}, f32[1,1,512]{2,1,0:T(1,128)}, u32[]{:S(2)}) copy-start(f32[1,1,512]{2,1,0:T(1,128)} %get-tuple-element.118) | copy-start | bytes 6148
  120.7 32.4 %copy-start.33 = (f32[1,1,512]{2,1,0:T(1,128)S(1)}, f32[1,1,512]{2,1,0:T(1,128)}, u32[]{:S(2)}) copy-start(f32[1,1,512]{2,1,0:T(1,128)} %get-tuple-element.119) | copy-start | bytes 6148
  120.7 32.4 %copy-start.34 = (f32[1,1,512]{2,1,0:T(1,128)S(1)}, f32[1,1,512]{2,1,0:T(1,128)}, u32[]{:S(2)}) copy-start(f32[1,1,512]{2,1,0:T(1,128)} %get-tuple-element.120) | copy-start | bytes 6148
  120.7 32.4 %copy-start.35 = (f32[1,1,512]{2,1,0:T(1,128)S(1)}, f32[1,1,512]{2,1,0:T(1,128)}, u32[]{:S(2)}) copy-start(f32[1,1,512]{2,1,0:T(1,128)} %get-tuple-element.121) | copy-start | bytes 6148
  120.7 32.4 %copy-start.36 = (f32[1,1,512]{2,1,0:T(1,128)S(1)}, f32[1,1,512]{2,1,0:T(1,128)}, u32[]{:S(2)}) copy-start(f32[1,1,512]{2,1,0:T(1,128)} %get-tuple-element.122) | copy-start | bytes 6148
  (76 other events, 921.9 us)
Sparse Core Ops, SparseCore 0:
  120.7 101.3 all-reduce.2
where the time goes:
time: 234 us; the launch traced here: 233 us
  waiting for transfers between devices  80.2 us (34%)
  starting transfers between devices  35 us (15%)
  blocking collectives  31.5 us (13%)
  local copies, waits for them, and re-layouts  25.9 us (11%)
  other arithmetic  25.8 us (11%)
  matrix products  19.2 us (8%)
  between operations  15.5 us (7%)
    psum x1, waiting for transfers between devices, on_device(): lax.psum((grad_weight, grad_out, grad_conv, grad_gain), ('lon', 'lat', 'd...  64.3 us
    psum x1, blocking collectives, on_device(): lax.psum((grad_weight, grad_out, grad_conv, grad_gain), ('lon', 'lat', 'd...  31.5 us
    reduce_sum x1, other arithmetic, on_device(): inverse = lax.rsqrt(jnp.mean(update * update, -1, keepdims=True) + EPSILON)  10.5 us
    ppermute x4, starting transfers between devices, with_halo(): before = lax.ppermute(last, axis, up)  9.14 us
    ppermute x4, starting transfers between devices, with_halo(): after = lax.ppermute(first, axis, down)  7.95 us
    all_to_all x1, waiting for transfers between devices, on_device(): lax.all_to_all(projected.reshape(batch_count, lat_rows, lon_cols, 3 * att...  6.17 us
    reduce_sum x3, other arithmetic, correlate(): pieces.append(jnp.sum(window * upstream, axis=(0, 1, 2)))  5.91 us
    unnamed x194, local copies, waits for them, and re-layouts  5.57 us
  transfers between devices with their start and end apart: 13, of which 6 were waited for; matrix products, arithmetic and copies ran while one was open for 19% of the time, Pallas kernels for 0%

commit v1 on v0

--- a/solution.py
+++ b/solution.py
@@ -168,7 +168,7 @@
         grad_update + spread(grad_padded, conv_weight[::-1, ::-1], lat_rows, lon_cols)
     ).astype(jnp.bfloat16)
     grad_conv = correlate(padded, grad_update, lat_rows, lon_cols)
-    totals = lax.psum((grad_weight, grad_out, grad_conv, grad_gain), ("lon", "lat", "dp"))
+    totals = lax.psum(lax.psum((grad_weight, grad_out, grad_conv, grad_gain), "lon"), ("lat", "dp"))
     return (result, grad_fields, totals[0], totals[1], totals[2], totals[3])
 
 

time: 234 us -> 270 us (1.15)
  waiting for transfers between devices: 80.2 us -> 129 us
  blocking collectives: 31.5 us -> 20 us
    psum x1 -> x2, waiting for transfers between devices: 64.3 us -> 106 us  [the longest x1 56.9 us: on_device(): lax.psum((grad_weight, grad_out, grad_conv, grad_gain), 'lon')]
    psum x1 -> x2, blocking collectives: 31.5 us -> 20 us  [the longest x1 13.2 us: on_device(): lax.psum((grad_weight, grad_out, grad_conv, grad_gain), 'lon')]
    another operation x1, local copies, waits for them, and re-layouts: 0.24 us -> 3.78 us  [correlate(): return jnp.stack(pieces).reshape(7, 7, -1)]
    unnamed x194 -> x168, local copies, waits for them, and re-layouts: 5.57 us -> 5.21 us
  transfers between devices with their start and end apart: 13 -> 14, of which waited for: 6 -> 7; matrix products, arithmetic and copies ran while one was open for 19% -> 13% of each run, Pallas kernels for 0% -> 0%
where the time goes in v1:
time: 270 us; the launch traced here: 269 us
  waiting for transfers between devices  129 us (48%)
  starting transfers between devices  34.7 us (13%)
  other arithmetic  25.4 us (9%)
  local copies, waits for them, and re-layouts  25.2 us (9%)
  blocking collectives  20 us (7%)
  matrix products  19.3 us (7%)
  between operations  15.3 us (6%)
    psum x1, waiting for transfers between devices, on_device(): lax.psum((grad_weight, grad_out, grad_conv, grad_gain), 'lon')  56.9 us
    psum x1, waiting for transfers between devices, on_device(): lax.psum(lax.psum((grad_weight, grad_out, grad_conv, grad_gain), 'lon'),...  48.8 us
    psum x1, blocking collectives, on_device(): lax.psum((grad_weight, grad_out, grad_conv, grad_gain), 'lon')  13.2 us
    reduce_sum x1, other arithmetic, on_device(): inverse = lax.rsqrt(jnp.mean(update * update, -1, keepdims=True) + EPSILON)  10.5 us
    ppermute x4, starting transfers between devices, with_halo(): before = lax.ppermute(last, axis, up)  8.72 us
    all_to_all x1, waiting for transfers between devices, on_device(): lax.all_to_all(projected.reshape(batch_count, lat_rows, lon_cols, 3 * att...  8.46 us
    ppermute x4, starting transfers between devices, with_halo(): after = lax.ppermute(first, axis, down)  7.94 us
    psum x1, blocking collectives, on_device(): lax.psum(lax.psum((grad_weight, grad_out, grad_conv, grad_gain), 'lon'),...  6.79 us
  transfers between devices with their start and end apart: 14, of which 7 were waited for; matrix products, arithmetic and copies ran while one was open for 13% of the time, Pallas kernels for 0%

profile of v1, /device:TPU:0, one launch (start us, length us, event | category | flops | bytes accessed | tf_op | source)
XLA Modules:
  0.0 268.8 jit_solution(4022623047159432627)
XLA Ops:
  8.4 3.1 %collective-permute-start = (bf16[1,32,3,512]{3,2,1,0:T(4,128)(2,1)S(1)}, bf16[1,32,3,512]{3,2,1,0:T(4,128)(2,1)S(1)}, u32[]{:S(2)}, u32[]{:S(2)}) collective-permute-start(bf16[1,32,3,512]{3,2,1,0:T(4,128)(2,1)S(1)} %get-tuple-element.96), channel_id=1, source_target_pairs={{0,4},{4,8},{8,12},{12,0},{1,5},{5,9},{9,13},{13,1},{2,6},{6,10},{... | collective-permute-start | bytes 294920 | tf_op jit(solution)/shard_map/ppermute | solution.py:18
  11.6 2.1 collective-permute-start.1
  13.6 1.9 fusion.15
  15.6 3.9 %all-to-all-start.2 = ((bf16[1,32,8,256]{3,2,0,1:T(8,128)(2,1)}), bf16[1,32,8,256]{3,2,0,1:T(8,128)(2,1)}, u32[]{:S(2)}, u32[]{:S(2)}) async-start(bf16[1,32,8,256]{3,2,0,1:T(8,128)(2,1)} %fusion.15), calls=%async_computation.2 | async-start | bytes 262144 | tf_op jit(solution)/shard_map/all_to_all | solution.py:140
  22.2 3.5 %collective-permute-start.2 = (bf16[1,3,14,512]{3,2,1,0:T(8,128)(2,1)S(1)}, bf16[1,3,14,512]{3,2,1,0:T(8,128)(2,1)S(1)}, u32[]{:S(2)}, u32[]{:S(2)}) collective-permute-start(bf16[1,3,14,512]{3,2,1,0:T(8,128)(2,1)S(1)} %get-tuple-element.87), channel_id=1, source_target_pairs={{0,2},{1,3},{4,6},{5,7},{8,10},{9,11},{12,14},{13,15},{16,18},{17,... | collective-permute-start | bytes 129032 | tf_op jit(solution)/shard_map/ppermute | solution.py:18
  27.7 4.0 %collective-permute-done.3 = bf16[1,3,14,512]{3,2,1,0:T(8,128)(2,1)S(1)} collective-permute-done((bf16[1,3,14,512]{3,2,1,0:T(8,128)(2,1)S(1)}, bf16[1,3,14,512]{3,2,1,0:T(8,128)(2,1)S(1)}, u32[]{:S(2)}, u32[]{:S(2)}) %collective-permute-start.3) | collective-permute-done | bytes 43040 | tf_op jit(solution)/shard_map/ppermute | solution.py:19
  32.1 1.9 slice_convert_fusion.2
  34.1 10.5 %multiply_reduce_fusion.51 = (f32[32,8]{1,0:T(8,128)S(1)}, f32[1,32,8,512]{3,2,1,0:T(8,128)S(1)}) fusion(f32[1,32,14,512]{3,2,1,0:T(8,128)S(1)} %get-tuple-element.80, f32[512]{0:T(512)} %bitcast.283, f32[512]{0:T(512)} %bitcast.285, f32[512]{0:T(512)S(1)} %bitcast.191, f32[512]{0:T(512)S(1)} %bitcast.193, f32[512]{0:T(512)S(1)} %bitcast.195, ...), kind=kLoop, calls=%fused_computation.293 | loop fusion | flops 13238016 | bytes 26577920 | tf_op jit(solution)/shard_map/reduce_sum | solution.py:119
  45.8 5.0 %all-to-all-start = ((bf16[1,32,8,768]{3,2,0,1:T(8,128)(2,1)}), bf16[1,32,8,768]{3,2,0,1:T(8,128)(2,1)S(1)}, u32[]{:S(2)}, u32[]{:S(2)}) async-start(bf16[1,32,8,768]{3,2,0,1:T(8,128)(2,1)} %fusion.10), calls=%async_computation | async-start | bytes 786432 | tf_op jit(solution)/shard_map/all_to_all | solution.py:123
  51.9 8.5 %all-to-all-done = bf16[1,32,8,768]{3,2,0,1:T(8,128)(2,1)S(1)} async-done(((bf16[1,32,8,768]{3,2,0,1:T(8,128)(2,1)}), bf16[1,32,8,768]{3,2,0,1:T(8,128)(2,1)S(1)}, u32[]{:S(2)}, u32[]{:S(2)}) %all-to-all-start) | async-done | bytes 393248 | tf_op jit(solution)/shard_map/all_to_all | solution.py:123
  61.7 2.1 fusion.164
  64.8 2.0 fusion.14
  66.8 1.8 fusion.11
  68.6 2.3 fusion.12
  74.2 3.9 %all-to-all-start.1 = ((bf16[1,8,32,256]{3,1,0,2:T(8,128)(2,1)}), bf16[1,8,32,256]{3,1,0,2:T(8,128)(2,1)}, u32[]{:S(2)}, u32[]{:S(2)}) async-start(bf16[1,8,32,256]{3,1,0,2:T(8,128)(2,1)} %reshape.619), calls=%async_computation.1 | async-start | bytes 262144 | tf_op jit(solution)/shard_map/all_to_all | solution.py:131
  78.2 2.3 fusion.13
  84.1 5.1 %all-to-all-start.3 = ((bf16[1,8,32,768]{3,1,0,2:T(8,128)(2,1)}), bf16[1,8,32,768]{3,1,0,2:T(8,128)(2,1)}, u32[]{:S(2)}, u32[]{:S(2)}) async-start(bf16[1,8,32,768]{3,1,0,2:T(8,128)(2,1)} %copy.93), calls=%async_computation.3 | async-start | bytes 786432 | tf_op jit(solution)/shard_map/all_to_all | solution.py:148
  93.1 5.1 %all-to-all-done.3 = bf16[1,8,32,768]{3,1,0,2:T(8,128)(2,1)} async-done(((bf16[1,8,32,768]{3,1,0,2:T(8,128)(2,1)}), bf16[1,8,32,768]{3,1,0,2:T(8,128)(2,1)}, u32[]{:S(2)}, u32[]{:S(2)}) %all-to-all-start.3) | async-done | bytes 393248 | tf_op jit(solution)/shard_map/all_to_all | solution.py:148
  100.4 1.6 fusion.139
  102.0 2.3 multiply_reduce_fusion.2
  104.3 2.0 multiply_reduce_fusion.29
  106.4 1.7 multiply_reduce_fusion.20
  108.1 3.8 %stack.199 = f32[49,512]{1,0:T(8,128)S(1)} concatenate(f32[1,512]{1,0:T(1,128)} %bitcast.333, f32[1,512]{1,0:T(1,128)} %bitcast.334, f32[1,512]{1,0:T(1,128)} %bitcast.335, f32[1,512]{1,0:T(1,128)} %bitcast.322, f32[1,512]{1,0:T(1,128)} %bitcast.321, f32[1,512]{1,0:T(1,128)} %bitcast.320, f32[1,512]{1,0:T(1,128)} %bitcast.319, f32[1,512]{1,0:T(1,128)} %bitcast.318, ...), dimensions={0} | concatenate | bytes 200704 | tf_op jit(solution)/shard_map/stack | solution.py:46
  113.4 3.3 %collective-permute-start.5 = (bf16[1,32,3,512]{3,2,1,0:T(4,128)(2,1)S(1)}, bf16[1,32,3,512]{3,2,1,0:T(4,128)(2,1)S(1)}, u32[]{:S(2)}, u32[]{:S(2)}) collective-permute-start(bf16[1,32,3,512]{3,2,1,0:T(4,128)(2,1)S(1)} %get-tuple-element.95), channel_id=1, source_target_pairs={{4,0},{8,4},{12,8},{0,12},{5,1},{9,5},{13,9},{1,13},{6,2},{10,6},{... | collective-permute-start | bytes 294920 | tf_op jit(solution)/shard_map/ppermute | solution.py:19
  116.6 3.1 %collective-permute-done.4 = bf16[1,32,3,512]{3,2,1,0:T(4,128)(2,1)S(1)} collective-permute-done((bf16[1,32,3,512]{3,2,1,0:T(4,128)(2,1)S(1)}, bf16[1,32,3,512]{3,2,1,0:T(4,128)(2,1)S(1)}, u32[]{:S(2)}, u32[]{:S(2)}) %collective-permute-start.4) | collective-permute-done | bytes 98336 | tf_op jit(solution)/shard_map/ppermute | solution.py:18
  119.7 2.3 collective-permute-done.5
  125.8 13.2 %psum.62 = f32[512]{0:T(512)S(1)} all-reduce(f32[512]{0:T(512)S(1)} %copy-done.78), channel_id=1, replica_groups=mesh['member'=2,'lon'=4,'lat'=2,'dp'=2] {'lon'}, use_global_device_ids=true, to_apply=%region_61.0 | all-reduce | flops 512 | bytes 4096 | tf_op jit(solution)/shard_map/psum | solution.py:171
  139.0 6.8 %psum.63 = f32[512]{0:T(512)} all-reduce(f32[512]{0:T(512)S(1)} %psum.62), channel_id=1, replica_groups=mesh['member'=2,'lon'=4,'lat'=2,'dp'=2] {'lat','dp'}, use_global_device_ids=true, to_apply=%region_62.0 | all-reduce | flops 512 | bytes 4096 | tf_op jit(solution)/shard_map/psum | solution.py:171
  145.8 56.9 %all-reduce.7.cloned.1.call-done = (f32[512,768]{1,0:T(8,128)}, f32[256,512]{1,0:T(8,128)}, f32[7,7,512]{2,1,0:T(8,128)}) async-done(((f32[512,768]{1,0:T(8,128)}, f32[256,512]{1,0:T(8,128)}, f32[7,7,512]{2,1,0:T(8,128)}), (f32[512,768]{1,0:T(8,128)}, f32[256,512]{1,0:T(8,128)}, f32[7,7,512]{2,1,0:T(8,128)})) %all-reduce.7.cloned.1.call-update) | async-done | bytes 2197520 | tf_op jit(solution)/shard_map/psum | solution.py:171
  203.8 5.2 %fusion.24 = bf16[1,32,8,512]{3,2,1,0:T(8,128)(2,1)} fusion(f32[1,32,8,512]{3,2,1,0:T(8,128)S(1)} %get-tuple-element.73, f32[1,38,14,512]{3,2,1,0:T(8,128)S(1)} %maximum_convert_fusion, f32[512]{0:T(512)} %bitcast.284, f32[512]{0:T(512)} %bitcast.286, f32[512]{0:T(512)S(1)} %bitcast.192, f32[512]{0:T(512)S(1)} %bitcast.194, f32[512]{0:T(512)S(1)} %bitcast.196, ...), kind=kLoop, calls=%fused_computation.42 | loop fusion | flops 12976128 | bytes 26576896 | tf_op jit(solution)/shard_map/convert_element_type | solution.py:169
  209.0 48.8 %all-reduce.5.cloned.1.call-done = (f32[512,768]{1,0:T(8,128)}, f32[256,512]{1,0:T(8,128)}, f32[7,7,512]{2,1,0:T(8,128)}) async-done(((f32[512,768]{1,0:T(8,128)}, f32[256,512]{1,0:T(8,128)}, f32[7,7,512]{2,1,0:T(8,128)}), (f32[512,768]{1,0:T(8,128)}, f32[256,512]{1,0:T(8,128)}, f32[7,7,512]{2,1,0:T(8,128)})) %all-reduce.5.cloned.1.call-update) | async-done | bytes 2197520 | tf_op jit(solution)/shard_map/psum | solution.py:171
  257.8 2.7 %copy.142 = f32[512,768]{1,0:T(8,128)} copy(f32[512,768]{1,0:T(8,128)} %get-tuple-element.157) | data formatting | bytes 3145728
  (222 shorter events, 30.6 us)
Async XLA Ops:
  7.2 37.5 %copy-start = (bf16[512,768]{1,0:T(8,128)(2,1)S(1)}, bf16[512,768]{1,0:T(8,128)(2,1)}, u32[]{:S(2)}) copy-start(bf16[512,768]{1,0:T(8,128)(2,1)} %param.10) | copy-start | bytes 2359300
  7.2 13.8 %copy-start.1 = (bf16[1,32,8,512]{3,2,1,0:T(8,128)(2,1)S(1)}, bf16[1,32,8,512]{3,2,1,0:T(8,128)(2,1)}, u32[]{:S(2)}) copy-start(bf16[1,32,8,512]{3,2,1,0:T(8,128)(2,1)} %param.6) | copy-start | bytes 786436
  7.2 12.3 %copy-start.17 = (f32[7,7,512]{2,1,0:T(8,128)S(1)}, f32[7,7,512]{2,1,0:T(8,128)}, u32[]{:S(2)}) copy-start(f32[7,7,512]{2,1,0:T(8,128)} %param.8) | copy-start | bytes 301060
  8.4 12.5 %collective-permute-start = (bf16[1,32,3,512]{3,2,1,0:T(4,128)(2,1)S(1)}, bf16[1,32,3,512]{3,2,1,0:T(4,128)(2,1)S(1)}, u32[]{:S(2)}, u32[]{:S(2)}) collective-permute-start(bf16[1,32,3,512]{3,2,1,0:T(4,128)(2,1)S(1)} %get-tuple-element.96), channel_id=1, source_target_pairs={{0,4},{4,8},{8,12},{12,0},{1,5},{5,9},{9,13},{13,1},{2,6},{6,10},{... | collective-permute-start | bytes 294920 | tf_op jit(solution)/shard_map/ppermute | solution.py:18
  11.6 9.4 %collective-permute-start.1 = (bf16[1,32,3,512]{3,2,1,0:T(4,128)(2,1)S(1)}, bf16[1,32,3,512]{3,2,1,0:T(4,128)(2,1)S(1)}, u32[]{:S(2)}, u32[]{:S(2)}) collective-permute-start(bf16[1,32,3,512]{3,2,1,0:T(4,128)(2,1)S(1)} %get-tuple-element.97), channel_id=1, source_target_pairs={{4,0},{8,4},{12,8},{0,12},{5,1},{9,5},{13,9},{1,13},{6,2},{10,6},{... | collective-permute-start | bytes 294920 | tf_op jit(solution)/shard_map/ppermute | solution.py:19
  15.6 30.2 %all-to-all-start.2 = ((bf16[1,32,8,256]{3,2,0,1:T(8,128)(2,1)}), bf16[1,32,8,256]{3,2,0,1:T(8,128)(2,1)}, u32[]{:S(2)}, u32[]{:S(2)}) async-start(bf16[1,32,8,256]{3,2,0,1:T(8,128)(2,1)} %fusion.15), calls=%async_computation.2 | async-start | bytes 262144 | tf_op jit(solution)/shard_map/all_to_all | solution.py:140
  20.2 13.8 %copy-start.19 = (f32[1,1,512]{2,1,0:T(1,128)}, f32[1,1,512]{2,1,0:T(1,128)S(1)}, u32[]{:S(2)}) copy-start(f32[1,1,512]{2,1,0:T(1,128)S(1)} %get-tuple-element.101) | copy-start | bytes 6148
  20.2 13.8 %copy-start.21 = (f32[1,1,512]{2,1,0:T(1,128)}, f32[1,1,512]{2,1,0:T(1,128)S(1)}, u32[]{:S(2)}) copy-start(f32[1,1,512]{2,1,0:T(1,128)S(1)} %get-tuple-element.102) | copy-start | bytes 6148
  20.2 13.8 %copy-start.23 = (f32[1,1,512]{2,1,0:T(1,128)}, f32[1,1,512]{2,1,0:T(1,128)S(1)}, u32[]{:S(2)}) copy-start(f32[1,1,512]{2,1,0:T(1,128)S(1)} %get-tuple-element.103) | copy-start | bytes 6148
  20.2 13.8 %copy-start.25 = (f32[1,1,512]{2,1,0:T(1,128)}, f32[1,1,512]{2,1,0:T(1,128)S(1)}, u32[]{:S(2)}) copy-start(f32[1,1,512]{2,1,0:T(1,128)S(1)} %get-tuple-element.104) | copy-start | bytes 6148
  20.2 13.8 %copy-start.27 = (f32[1,1,512]{2,1,0:T(1,128)}, f32[1,1,512]{2,1,0:T(1,128)S(1)}, u32[]{:S(2)}) copy-start(f32[1,1,512]{2,1,0:T(1,128)S(1)} %get-tuple-element.105) | copy-start | bytes 6148
  20.2 13.8 %copy-start.29 = (f32[1,1,512]{2,1,0:T(1,128)}, f32[1,1,512]{2,1,0:T(1,128)S(1)}, u32[]{:S(2)}) copy-start(f32[1,1,512]{2,1,0:T(1,128)S(1)} %get-tuple-element.106) | copy-start | bytes 6148
  20.2 13.8 %copy-start.31 = (f32[1,1,512]{2,1,0:T(1,128)}, f32[1,1,512]{2,1,0:T(1,128)S(1)}, u32[]{:S(2)}) copy-start(f32[1,1,512]{2,1,0:T(1,128)S(1)} %get-tuple-element.107) | copy-start | bytes 6148
  20.2 13.8 %copy-start.33 = (f32[1,1,512]{2,1,0:T(1,128)}, f32[1,1,512]{2,1,0:T(1,128)S(1)}, u32[]{:S(2)}) copy-start(f32[1,1,512]{2,1,0:T(1,128)S(1)} %get-tuple-element.108) | copy-start | bytes 6148
  20.2 13.8 %copy-start.35 = (f32[1,1,512]{2,1,0:T(1,128)}, f32[1,1,512]{2,1,0:T(1,128)S(1)}, u32[]{:S(2)}) copy-start(f32[1,1,512]{2,1,0:T(1,128)S(1)} %get-tuple-element.109) | copy-start | bytes 6148
  20.2 13.8 %copy-start.37 = (f32[1,1,512]{2,1,0:T(1,128)}, f32[1,1,512]{2,1,0:T(1,128)S(1)}, u32[]{:S(2)}) copy-start(f32[1,1,512]{2,1,0:T(1,128)S(1)} %get-tuple-element.110) | copy-start | bytes 6148
  20.9 11.2 %copy-start.6 = (bf16[1,32,3,512]{3,2,1,0:T(4,128)(2,1)}, bf16[1,32,3,512]{3,2,1,0:T(4,128)(2,1)S(1)}, u32[]{:S(2)}) copy-start(bf16[1,32,3,512]{3,2,1,0:T(4,128)(2,1)S(1)} %collective-permute-done) | copy-start | bytes 294916
  21.0 11.1 %copy-start.8 = (bf16[1,32,3,512]{3,2,1,0:T(4,128)(2,1)}, bf16[1,32,3,512]{3,2,1,0:T(4,128)(2,1)S(1)}, u32[]{:S(2)}) copy-start(bf16[1,32,3,512]{3,2,1,0:T(4,128)(2,1)S(1)} %collective-permute-done.1) | copy-start | bytes 294916
  22.2 5.5 %collective-permute-start.2 = (bf16[1,3,14,512]{3,2,1,0:T(8,128)(2,1)S(1)}, bf16[1,3,14,512]{3,2,1,0:T(8,128)(2,1)S(1)}, u32[]{:S(2)}, u32[]{:S(2)}) collective-permute-start(bf16[1,3,14,512]{3,2,1,0:T(8,128)(2,1)S(1)} %get-tuple-element.87), channel_id=1, source_target_pairs={{0,2},{1,3},{4,6},{5,7},{8,10},{9,11},{12,14},{13,15},{16,18},{17,... | collective-permute-start | bytes 129032 | tf_op jit(solution)/shard_map/ppermute | solution.py:18
  25.8 6.0 %collective-permute-start.3 = (bf16[1,3,14,512]{3,2,1,0:T(8,128)(2,1)S(1)}, bf16[1,3,14,512]{3,2,1,0:T(8,128)(2,1)S(1)}, u32[]{:S(2)}, u32[]{:S(2)}) collective-permute-start(bf16[1,3,14,512]{3,2,1,0:T(8,128)(2,1)S(1)} %get-tuple-element.88), channel_id=1, source_target_pairs={{2,0},{3,1},{6,4},{7,5},{10,8},{11,9},{14,12},{15,13},{18,16},{19,... | collective-permute-start | bytes 129032 | tf_op jit(solution)/shard_map/ppermute | solution.py:19
  45.8 14.6 %all-to-all-start = ((bf16[1,32,8,768]{3,2,0,1:T(8,128)(2,1)}), bf16[1,32,8,768]{3,2,0,1:T(8,128)(2,1)S(1)}, u32[]{:S(2)}, u32[]{:S(2)}) async-start(bf16[1,32,8,768]{3,2,0,1:T(8,128)(2,1)} %fusion.10), calls=%async_computation | async-start | bytes 786432 | tf_op jit(solution)/shard_map/all_to_all | solution.py:123
  74.2 9.9 %all-to-all-start.1 = ((bf16[1,8,32,256]{3,1,0,2:T(8,128)(2,1)}), bf16[1,8,32,256]{3,1,0,2:T(8,128)(2,1)}, u32[]{:S(2)}, u32[]{:S(2)}) async-start(bf16[1,8,32,256]{3,1,0,2:T(8,128)(2,1)} %reshape.619), calls=%async_computation.1 | async-start | bytes 262144 | tf_op jit(solution)/shard_map/all_to_all | solution.py:131
  84.1 14.1 %all-to-all-start.3 = ((bf16[1,8,32,768]{3,1,0,2:T(8,128)(2,1)}), bf16[1,8,32,768]{3,1,0,2:T(8,128)(2,1)}, u32[]{:S(2)}, u32[]{:S(2)}) async-start(bf16[1,8,32,768]{3,1,0,2:T(8,128)(2,1)} %copy.93), calls=%async_computation.3 | async-start | bytes 786432 | tf_op jit(solution)/shard_map/all_to_all | solution.py:148
  89.3 113.5 %all-reduce.7.cloned.1.call-start = ((), (), s32[]{:S(2)}) async-start(), calls=%async_computation.5 | async-start | bytes 4423680 | tf_op jit(solution)/shard_map/psum | solution.py:171
  112.6 12.2 %copy-start.10 = (bf16[1,4,8,8,256]{4,3,2,1,0:T(8,128)(2,1)S(1)}, bf16[1,4,8,8,256]{4,3,2,1,0:T(8,128)(2,1)}, u32[]{:S(2)}) copy-start(bf16[1,4,8,8,256]{4,3,2,1,0:T(8,128)(2,1)} %copy-done.9) | copy-start | bytes 393220
  112.6 12.3 %copy-start.11 = (bf16[256,512]{1,0:T(8,128)(2,1)S(1)}, bf16[256,512]{1,0:T(8,128)(2,1)}, u32[]{:S(2)}) copy-start(bf16[256,512]{1,0:T(8,128)(2,1)} %param.11) | copy-start | bytes 786436
  112.6 13.2 %copy-start.78 = (f32[512]{0:T(512)S(1)}, f32[512]{0:T(512)}, u32[]{:S(2)}) copy-start(f32[512]{0:T(512)} %get-tuple-element.48) | copy-start | bytes 6148
  112.6 145.2 %all-reduce.5.cloned.1.call-start = ((), (), s32[]{:S(2)}) async-start(), calls=%async_computation.4 | async-start | bytes 4423680 | tf_op jit(solution)/shard_map/psum | solution.py:171
  112.8 7.0 %collective-permute-start.4 = (bf16[1,32,3,512]{3,2,1,0:T(4,128)(2,1)S(1)}, bf16[1,32,3,512]{3,2,1,0:T(4,128)(2,1)S(1)}, u32[]{:S(2)}, u32[]{:S(2)}) collective-permute-start(bf16[1,32,3,512]{3,2,1,0:T(4,128)(2,1)S(1)} %get-tuple-element.94), channel_id=1, source_target_pairs={{0,4},{4,8},{8,12},{12,0},{1,5},{5,9},{9,13},{13,1},{2,6},{6,10},{... | collective-permute-start | bytes 294920 | tf_op jit(solution)/shard_map/ppermute | solution.py:18
  113.4 8.6 %collective-permute-start.5 = (bf16[1,32,3,512]{3,2,1,0:T(4,128)(2,1)S(1)}, bf16[1,32,3,512]{3,2,1,0:T(4,128)(2,1)S(1)}, u32[]{:S(2)}, u32[]{:S(2)}) collective-permute-start(bf16[1,32,3,512]{3,2,1,0:T(4,128)(2,1)S(1)} %get-tuple-element.95), channel_id=1, source_target_pairs={{4,0},{8,4},{12,8},{0,12},{5,1},{9,5},{13,9},{1,13},{6,2},{10,6},{... | collective-permute-start | bytes 294920 | tf_op jit(solution)/shard_map/ppermute | solution.py:19
  122.1 81.1 %collective-permute-start.6 = (bf16[1,3,14,512]{3,2,1,0:T(8,128)(2,1)S(1)}, bf16[1,3,14,512]{3,2,1,0:T(8,128)(2,1)S(1)}, u32[]{:S(2)}, u32[]{:S(2)}) collective-permute-start(bf16[1,3,14,512]{3,2,1,0:T(8,128)(2,1)S(1)} %get-tuple-element.83), channel_id=1, source_target_pairs={{0,2},{1,3},{4,6},{5,7},{8,10},{9,11},{12,14},{13,15},{16,18},{17,... | collective-permute-start | bytes 129032 | tf_op jit(solution)/shard_map/ppermute | solution.py:18
  123.5 79.7 %collective-permute-start.7 = (bf16[1,3,14,512]{3,2,1,0:T(8,128)(2,1)S(1)}, bf16[1,3,14,512]{3,2,1,0:T(8,128)(2,1)S(1)}, u32[]{:S(2)}, u32[]{:S(2)}) collective-permute-start(bf16[1,3,14,512]{3,2,1,0:T(8,128)(2,1)S(1)} %get-tuple-element.84), channel_id=1, source_target_pairs={{2,0},{3,1},{6,4},{7,5},{10,8},{11,9},{14,12},{15,13},{18,16},{19,... | collective-permute-start | bytes 129032 | tf_op jit(solution)/shard_map/ppermute | solution.py:19
  (64 other events, 106.1 us)
Sparse Core Ops, SparseCore 0:
  112.7 89.9 all-reduce.6
  205.3 52.4 all-reduce.4
